TPU v7x, 512 devices: a whole 4x8x8 slice. The times are simulated.
512 devices in a mesh: section: 8 (over x, core), dp: 64 (over z, y).
Axes of the slice: x: 4, y: 8, z: 8, core: 2. Of those that a mesh axis runs over, the one named last changes fastest.
Arguments:
- inputs: bfloat16 [8, 1024, 4096], P(None, 'dp')
- cotangent: bfloat16 [8, 1024, 4096], P(None, 'dp'), may hold values from -0.59765625 to 0.59765625
- row_adapter_slot: int32 [8, 1024], P(None, 'dp'), may hold values from 0 to 1
- deployed_adapter_ids: int32 [64, 2], replicated, may hold values from 0 to 63, as said below
- adapter_owner_device: int32 [64], replicated, may hold values from 0 to 63, each once
- adapter_down_weight: bfloat16 [8, 1, 64, 2, 32, 4096], P('section', None, 'dp'), as said below
- adapter_up_weight: bfloat16 [8, 1, 64, 2, 32, 4096], P('section', None, 'dp'), as said below
Outputs:
- grad_down: float32 [8, 1, 64, 32, 4096], P('section', None, 'dp')
- grad_up: float32 [8, 1, 64, 32, 4096], P('section', None, 'dp')
Inputs may be any that keep to these rules, and one draw needn't show every extreme that they name: `deployed_adapter_ids`: the 2 adapter ids of one device differ, and every adapter is deployed on at least one device; some adapters are deployed on many devices. `adapter_owner_device`: every data device owns exactly one adapter. `adapter_down_weight`: copies of the same adapter on different devices are equal. `adapter_up_weight`: copies of the same adapter on different devices are equal.
All inputs are finite; a program needn't handle non-finite values.
Results may differ from a plain program's by a relative error of at most 0.0086.
Values may be sent and summed in bfloat16 or wider, within the bound.
A program may use at most 64 MiB of HBM per device.

v0:
```python
import jax
import jax.numpy as jnp
from jax import lax
from jax.sharding import PartitionSpec as P

adapter_scale = 0.5
epsilon = 1e-06


def from_behind(block, axis, distance):
    devices = range(lax.axis_size(axis))
    route = [(i - distance, i) for i in devices if i - distance in devices]
    return lax.ppermute(block, axis, route)


def norm_parts(hidden_state):
    value_rows = hidden_state.astype(jnp.float32)
    inverse = lax.rsqrt(jnp.mean(value_rows * value_rows, axis=-1, keepdims=True) + epsilon)
    return (inverse, value_rows * inverse)


def layer_forward(hidden_state, down_weight, up_weight, row_mask):
    inverse, unit = norm_parts(hidden_state)
    normed = unit.astype(jnp.bfloat16)
    rank_complete = lax.dot_general(
        normed, down_weight, (((1,), (1,)), ((), ())), preferred_element_type=jnp.float32
    )
    rank_row_values = jnp.where(row_mask, rank_complete, 0.0).astype(jnp.bfloat16)
    row_updates = jnp.dot(rank_row_values, up_weight, preferred_element_type=jnp.float32)
    return (
        (hidden_state.astype(jnp.float32) + adapter_scale * row_updates).astype(jnp.bfloat16),
        rank_row_values,
    )


def layer_backward(hidden_state, grad_rows, down_weight, up_weight, row_mask):
    inverse, unit = norm_parts(hidden_state)
    normed = unit.astype(jnp.bfloat16)
    rank_complete = adapter_scale * lax.dot_general(
        grad_rows, up_weight, (((1,), (1,)), ((), ())), preferred_element_type=jnp.float32
    )
    rank_grads = jnp.where(row_mask, rank_complete, 0.0).astype(jnp.bfloat16)
    unit_grads = jnp.dot(rank_grads, down_weight, preferred_element_type=jnp.float32)
    back_rows = grad_rows.astype(jnp.float32) + inverse * (
        unit_grads - unit * jnp.mean(unit_grads * unit, axis=-1, keepdims=True)
    )
    return (back_rows.astype(jnp.bfloat16), normed, rank_grads)


def put_block(store, layer_idx, position, value, usable):
    previous = store[layer_idx, position]
    return store.at[layer_idx, position].set(jnp.where(usable, value, previous))


def body(
    inputs,
    cotangent,
    row_adapter_slot,
    deployed_adapter_ids,
    adapter_owner_device,
    adapter_down_weight,
    adapter_up_weight,
):
    sections = lax.axis_size("section")
    section_index = lax.axis_index("section")
    pieces = lax.axis_size("dp")
    micro_count, row_count, feature_rows = inputs.shape
    layer_stack = adapter_down_weight.shape[1]
    adapter_slot_count = adapter_down_weight.shape[3]
    rank_length = adapter_down_weight.shape[4]
    rank_columns = adapter_slot_count * rank_length
    piece_cols = feature_rows // pieces
    down_weight = adapter_down_weight.reshape(layer_stack, rank_columns, feature_rows)
    up_weight = adapter_up_weight.reshape(layer_stack, rank_columns, feature_rows)
    column_slot = jnp.arange(rank_columns, dtype=jnp.int32) // rank_length
    masks = row_adapter_slot[..., None] == column_slot
    step_count = micro_count + sections - 1
    ticks = jnp.arange(step_count, dtype=jnp.int32)

    def forward_tick(carried, tick_now):
        incoming, saved_in, saved_rank = carried
        micro_index = tick_now - section_index
        usable = (micro_index >= 0) & (micro_index < micro_count)
        position = jnp.clip(micro_index, 0, micro_count - 1)
        hidden_state = jnp.where(section_index == 0, inputs[position], incoming)
        row_mask = masks[position]
        saved_in = put_block(saved_in, 0, position, hidden_state, usable)
        hidden_state, rank_row_values = layer_forward(
            hidden_state, down_weight[0], up_weight[0], row_mask
        )
        saved_rank = put_block(saved_rank, 0, position, rank_row_values, usable)
        incoming = from_behind(hidden_state, "section", 1)
        return ((incoming, saved_in, saved_rank), None)

    start_forward = (
        jnp.zeros((row_count, feature_rows), jnp.bfloat16),
        jnp.zeros((layer_stack, micro_count, row_count, feature_rows), jnp.bfloat16),
        jnp.zeros((layer_stack, micro_count, row_count, rank_columns), jnp.bfloat16),
    )
    (unused_rows, saved_in, saved_rank), unused_out = lax.scan(forward_tick, start_forward, ticks)
    records = (
        jnp.zeros((layer_stack, micro_count, row_count, feature_rows), jnp.bfloat16),
        jnp.zeros((layer_stack, micro_count, row_count, rank_columns), jnp.bfloat16),
    )

    def backward_tick(carried, tick_now):
        incoming, records = carried
        micro_index = tick_now - (sections - 1 - section_index)
        usable = (micro_index >= 0) & (micro_index < micro_count)
        position = jnp.clip(micro_index, 0, micro_count - 1)
        grad_rows = jnp.where(section_index == sections - 1, cotangent[position], incoming)
        row_mask = masks[position]
        for layer_idx in reversed(range(layer_stack)):
            hidden_state = saved_in[layer_idx, position]
            rank_row_values = saved_rank[layer_idx, position]
            back_rows, normed, rank_grads = layer_backward(
                hidden_state, grad_rows, down_weight[layer_idx], up_weight[layer_idx], row_mask
            )
            records = (
                put_block(records[0], layer_idx, position, grad_rows, usable),
                put_block(records[1], layer_idx, position, rank_grads, usable),
            )
            grad_rows = back_rows
        incoming = from_behind(grad_rows, "section", -1)
        return ((incoming, records), None)

    start_backward = (jnp.zeros((row_count, feature_rows), jnp.bfloat16), records)
    (unused_grads, records), unused_out = lax.scan(backward_tick, start_backward, ticks)
    token_count = micro_count * row_count
    normed_all = (
        norm_parts(saved_in)[1]
        .astype(jnp.bfloat16)
        .reshape(layer_stack, token_count, pieces, piece_cols)
    )
    grads_all = records[0].reshape(layer_stack, token_count, pieces, piece_cols)
    normed_recv, grads_recv = (
        lax.all_to_all(normed_all, "dp", split_axis=2, concat_axis=1, tiled=True),
        lax.all_to_all(grads_all, "dp", split_axis=2, concat_axis=1, tiled=True),
    )
    normed_recv = normed_recv.reshape(layer_stack, pieces, token_count, piece_cols)
    grads_recv = grads_recv.reshape(layer_stack, pieces, token_count, piece_cols)
    rank_local = saved_rank.reshape(layer_stack, token_count, rank_columns)
    rank_grad_local = records[1].reshape(layer_stack, token_count, rank_columns)
    rank_every, rank_grad_every = (
        lax.all_gather(rank_local, "dp", axis=1, tiled=True),
        lax.all_gather(rank_grad_local, "dp", axis=1, tiled=True),
    )
    rank_every = rank_every.reshape(layer_stack, pieces, token_count, rank_columns)
    rank_grad_every = rank_grad_every.reshape(layer_stack, pieces, token_count, rank_columns)
    pieces_down = jnp.einsum(
        "lstk,lstc->slkc", rank_grad_every, normed_recv, preferred_element_type=jnp.float32
    )
    up_gradient_pieces = adapter_scale * jnp.einsum(
        "lstk,lstc->slkc", rank_every, grads_recv, preferred_element_type=jnp.float32
    )
    pieces_down = pieces_down.reshape(
        pieces, layer_stack, adapter_slot_count, rank_length * piece_cols
    )
    up_gradient_pieces = up_gradient_pieces.reshape(
        pieces, layer_stack, adapter_slot_count, rank_length * piece_cols
    )
    adapters = adapter_owner_device.shape[0]
    adapter_ids = jnp.arange(adapters, dtype=jnp.int32)
    owner_of = jnp.sum(
        jnp.where(deployed_adapter_ids[..., None] == adapter_ids, adapter_owner_device, 0), axis=-1
    )
    owner_ids = jnp.arange(pieces, dtype=jnp.int32)
    select = (owner_of[None, :, :] == owner_ids[:, None, None]).astype(jnp.float32)
    owned_down = jnp.einsum("osk,slkx->olx", select, pieces_down, precision=lax.Precision.HIGHEST)
    owned_up = jnp.einsum(
        "osk,slkx->olx", select, up_gradient_pieces, precision=lax.Precision.HIGHEST
    )
    owned_down = owned_down.reshape(pieces, layer_stack, rank_length, piece_cols)
    owned_up = owned_up.reshape(pieces, layer_stack, rank_length, piece_cols)
    final_down, final_up = (
        lax.all_to_all(
            owned_down.astype(jnp.bfloat16), "dp", split_axis=0, concat_axis=3, tiled=True
        ).astype(owned_down.dtype),
        lax.all_to_all(
            owned_up.astype(jnp.bfloat16), "dp", split_axis=0, concat_axis=3, tiled=True
        ).astype(owned_up.dtype),
    )
    grad_down = final_down.reshape(1, layer_stack, 1, rank_length, feature_rows)
    grad_up = final_up.reshape(1, layer_stack, 1, rank_length, feature_rows)
    return (grad_down, grad_up)


def solution(mesh):
    placed = (
        P(None, "dp", None),
        P(None, "dp", None),
        P(None, "dp"),
        P(),
        P(),
        P("section", None, "dp", None, None, None),
        P("section", None, "dp", None, None, None),
    )
    return jax.shard_map(
        body,
        mesh=mesh,
        in_specs=placed,
        out_specs=(P("section", None, "dp", None, None), P("section", None, "dp", None, None)),
        check_vma=False,
    )
```

profile of v0, /device:TPU:2, one launch (start us, length us, event | category | flops | bytes accessed | tf_op | source)
XLA Modules:
  0.0 656.7 jit_solution(1103574373725658941)
XLA Ops:
  8.2 210.1 %while.35 = (s32[]{:T(128)}, bf16[16,4096]{1,0:T(8,128)(2,1)S(1)}, bf16[1,8,16,4096]{3,2,1,0:T(8,128)(2,1)S(1)}, bf16[1,8,16,64]{3,2,1,0:T(8,128)(2,1)S(1)}, pre...) while((s32[]{:T(128)}, bf16[16,4096]{1,0:T(8,128)(2,1)S(1)}, ...), condition=%wide.region_4.5_spmd, body=%wide.region_1.4_spmd.sunk | while | flops 17633332 | bytes 3036152 | solution.py:100
  17.8 4.4 collective-permute-done
  31.8 4.4 collective-permute-done
  45.9 4.4 collective-permute-done
  59.9 4.4 collective-permute-done
  73.9 4.4 collective-permute-done
  87.9 4.4 collective-permute-done
  101.9 4.4 collective-permute-done
  115.9 4.4 collective-permute-done
  129.9 4.4 collective-permute-done
  143.9 4.4 collective-permute-done
  157.9 4.4 collective-permute-done
  171.9 4.4 collective-permute-done
  185.9 4.4 collective-permute-done
  199.9 4.4 collective-permute-done
  213.9 4.4 collective-permute-done
  218.4 192.8 %while.36 = (s32[]{:T(128)}, bf16[16,4096]{1,0:T(8,128)(2,1)S(1)}, bf16[1,8,16,4096]{3,2,1,0:T(8,128)(2,1)S(1)}, bf16[1,8,16,64]{3,2,1,0:T(8,128)(2,1)S(1)}, pre...) while((s32[]{:T(128)}, bf16[16,4096]{1,0:T(8,128)(2,1)S(1)}, ...), condition=%wide.region_9.10_spmd, body=%wide.region_5.9_spmd.sunk | while | flops 17962036 | bytes 5919656 | solution.py:128
  236.2 3.8 collective-permute-start.1
  240.0 2.5 collective-permute-done.1
  249.2 3.8 collective-permute-start.1
  262.2 3.8 collective-permute-start.1
  266.0 2.5 collective-permute-done.1
  275.1 3.8 collective-permute-start.1
  278.9 2.5 collective-permute-done.1
  288.1 3.8 collective-permute-start.1
  291.9 2.5 collective-permute-done.1
  301.1 3.8 collective-permute-start.1
  314.1 3.8 collective-permute-start.1
  327.0 3.8 collective-permute-start.1
  330.8 2.5 collective-permute-done.1
  340.0 3.8 collective-permute-start.1
  353.0 3.8 collective-permute-start.1
  366.0 3.8 collective-permute-start.1
  378.9 3.8 collective-permute-start.1
  391.9 3.8 collective-permute-start.1
  404.9 3.8 collective-permute-start.1
  413.5 3.3 reshape.319
  416.8 2.9 copy.52
  419.7 16.8 %all-to-all-start = ((bf16[1,128,64,64]{1,3,0,2:T(8,128)(2,1)}), bf16[1,128,64,64]{1,3,0,2:T(8,128)(2,1)}, u32[]{:S(2)}, u32[]{:S(2)}) async-start(bf16[1,128,64,64]{1,3,0,2:T(8,128)(2,1)} %copy.52), calls=%async_computation | async-start | bytes 2097152 | tf_op jit(solution)/shard_map/all_to_all | solution.py:137
  439.6 2.9 copy.59
  442.5 24.1 %all-to-all-done = bf16[1,128,64,64]{1,3,0,2:T(8,128)(2,1)} async-done(((bf16[1,128,64,64]{1,3,0,2:T(8,128)(2,1)}), bf16[1,128,64,64]{1,3,0,2:T(8,128)(2,1)}, u32[]{:S(2)}, u32[]{:S(2)}) %all-to-all-start) | async-done | bytes 1048608 | tf_op jit(solution)/shard_map/all_to_all | solution.py:137
  466.6 8.4 %all-to-all-start.2 = ((bf16[1,128,64,64]{1,3,0,2:T(8,128)(2,1)}), bf16[1,128,64,64]{1,3,0,2:T(8,128)(2,1)}, u32[]{:S(2)}, u32[]{:S(2)}) async-start(bf16[1,128,64,64]{1,3,0,2:T(8,128)(2,1)} %copy.59), calls=%async_computation.2 | async-start | bytes 2097152 | tf_op jit(solution)/shard_map/all_to_all | solution.py:138
  475.2 46.8 %all-gather.3.cloned.1.call-done = bf16[1,8192,64]{1,2,0:T(8,128)(2,1)} async-done(((bf16[1,128,64]{1,2,0:T(8,128)(2,1)}), bf16[1,8192,64]{1,2,0:T(8,128)(2,1)}) %all-gather.3.cloned.1.call-update) | async-done | bytes 1048592 | tf_op jit(solution)/shard_map/all_gather | solution.py:146
  534.0 67.8 %all-gather.5.cloned.1.call-done = bf16[1,8192,64]{1,2,0:T(8,128)(2,1)} async-done(((bf16[1,128,64]{1,2,0:T(8,128)(2,1)}), bf16[1,8192,64]{1,2,0:T(8,128)(2,1)}) %all-gather.5.cloned.1.call-update) | async-done | bytes 1048592 | tf_op jit(solution)/shard_map/all_gather | solution.py:145
  603.2 8.0 %all-to-all-start.1 = ((bf16[64,2,1024]{2,1,0:T(2,128)(2,1)}), bf16[64,2,1024]{2,1,0:T(2,128)(2,1)S(1)}, u32[]{:S(2)}, u32[]{:S(2)}) async-start(bf16[64,2,1024]{2,1,0:T(2,128)(2,1)} %reshape.335), calls=%async_computation.1 | async-start | bytes 524288 | tf_op jit(solution)/shard_map/all_to_all | solution.py:176
  621.6 3.0 all-to-all-done.1
  624.6 9.5 %all-to-all-start.3 = ((bf16[64,2,1024]{2,1,0:T(2,128)(2,1)}), bf16[64,2,1024]{2,1,0:T(2,128)(2,1)S(1)}, u32[]{:S(2)}, u32[]{:S(2)}) async-start(bf16[64,2,1024]{2,1,0:T(2,128)(2,1)} %reshape.337), calls=%async_computation.3 | async-start | bytes 524288 | tf_op jit(solution)/shard_map/all_to_all | solution.py:179
  636.3 11.3 %all-to-all-done.3 = bf16[64,2,1024]{2,1,0:T(2,128)(2,1)S(1)} async-done(((bf16[64,2,1024]{2,1,0:T(2,128)(2,1)}), bf16[64,2,1024]{2,1,0:T(2,128)(2,1)S(1)}, u32[]{:S(2)}, u32[]{:S(2)}) %all-to-all-start.3) | async-done | bytes 262176 | tf_op jit(solution)/shard_map/all_to_all | solution.py:179
  (406 shorter events, 285.9 us)
Async XLA Ops:
  7.2 514.8 %all-gather.3.cloned.1.call-start = ((), (), s32[]{:S(2)}) async-start(), calls=%async_computation.4 | async-start | bytes 1064960 | tf_op jit(solution)/shard_map/all_gather | solution.py:146
  15.9 6.3 collective-permute-start
  29.9 6.4 collective-permute-start
  44.0 6.3 collective-permute-start
  58.0 6.3 collective-permute-start
  72.0 6.3 collective-permute-start
  86.0 6.3 collective-permute-start
  100.0 6.3 collective-permute-start
  114.0 6.3 collective-permute-start
  128.0 6.3 collective-permute-start
  142.0 6.3 collective-permute-start
  156.0 6.3 collective-permute-start
  170.0 6.3 collective-permute-start
  184.0 6.3 collective-permute-start
  198.0 6.3 collective-permute-start
  212.0 6.3 collective-permute-start
  218.4 6.2 copy-start
  225.1 4.4 collective-permute-start.1
  229.5 6.2 copy-start
  236.2 6.3 collective-permute-start.1
  242.5 6.2 copy-start
  249.2 6.3 collective-permute-start.1
  255.5 6.2 copy-start
  262.2 6.3 collective-permute-start.1
  268.5 6.2 copy-start
  275.1 6.3 collective-permute-start.1
  288.1 6.3 collective-permute-start.1
  294.4 6.2 copy-start
  301.1 6.3 collective-permute-start.1
  307.4 6.2 copy-start
  314.1 6.3 collective-permute-start.1
  320.4 6.2 copy-start
  327.0 6.3 collective-permute-start.1
  333.3 6.2 copy-start
  340.0 6.3 collective-permute-start.1
  346.3 6.2 copy-start
  353.0 6.3 collective-permute-start.1
  366.0 6.3 collective-permute-start.1
  378.9 6.3 collective-permute-start.1
  391.9 6.3 collective-permute-start.1
  404.9 6.3 collective-permute-start.1
  419.7 46.9 %all-to-all-start = ((bf16[1,128,64,64]{1,3,0,2:T(8,128)(2,1)}), bf16[1,128,64,64]{1,3,0,2:T(8,128)(2,1)}, u32[]{:S(2)}, u32[]{:S(2)}) async-start(bf16[1,128,64,64]{1,3,0,2:T(8,128)(2,1)} %copy.52), calls=%async_computation | async-start | bytes 2097152 | tf_op jit(solution)/shard_map/all_to_all | solution.py:137
  436.5 165.3 %all-gather.5.cloned.1.call-start = ((), (), s32[]{:S(2)}) async-start(), calls=%async_computation.5 | async-start | bytes 1064960 | tf_op jit(solution)/shard_map/all_gather | solution.py:145
  439.5 35.4 %copy-start.1 = (s32[64,2]{0,1:T(2,128)S(1)}, s32[64,2]{0,1:T(2,128)}, u32[]{:S(2)}) copy-start(s32[64,2]{0,1:T(2,128)} %param.22) | copy-start | bytes 1540
  439.5 35.4 %copy-start.2 = (s32[64]{0:T(128)S(1)}, s32[64]{0:T(128)}, u32[]{:S(2)}) copy-start(s32[64]{0:T(128)} %param.23) | copy-start | bytes 772
  466.6 136.7 %all-to-all-start.2 = ((bf16[1,128,64,64]{1,3,0,2:T(8,128)(2,1)}), bf16[1,128,64,64]{1,3,0,2:T(8,128)(2,1)}, u32[]{:S(2)}, u32[]{:S(2)}) async-start(bf16[1,128,64,64]{1,3,0,2:T(8,128)(2,1)} %copy.59), calls=%async_computation.2 | async-start | bytes 2097152 | tf_op jit(solution)/shard_map/all_to_all | solution.py:138
  603.2 21.4 %all-to-all-start.1 = ((bf16[64,2,1024]{2,1,0:T(2,128)(2,1)}), bf16[64,2,1024]{2,1,0:T(2,128)(2,1)S(1)}, u32[]{:S(2)}, u32[]{:S(2)}) async-start(bf16[64,2,1024]{2,1,0:T(2,128)(2,1)} %reshape.335), calls=%async_computation.1 | async-start | bytes 524288 | tf_op jit(solution)/shard_map/all_to_all | solution.py:176
  624.6 23.1 %all-to-all-start.3 = ((bf16[64,2,1024]{2,1,0:T(2,128)(2,1)}), bf16[64,2,1024]{2,1,0:T(2,128)(2,1)S(1)}, u32[]{:S(2)}, u32[]{:S(2)}) async-start(bf16[64,2,1024]{2,1,0:T(2,128)(2,1)} %reshape.337), calls=%async_computation.3 | async-start | bytes 524288 | tf_op jit(solution)/shard_map/all_to_all | solution.py:179
  (5 other events, 31.1 us)
Sparse Core Ops, SparseCore 0:
  412.0 109.9 all-gather.2
  525.5 76.1 all-gather.4
where the time goes:
time: 662 us; the launch traced here: 657 us
  waiting for transfers between devices  256 us (39%)
  starting transfers between devices  126 us (19%)
  other arithmetic  98.3 us (15%)
  matrix products  89.6 us (14%)
  local copies, waits for them, and re-layouts  51.3 us (8%)
  loops' own time  21 us (3%)
  between operations  14.3 us (2%)
    ppermute x30, waiting for transfers between devices, from_behind(): return lax.ppermute(block, axis, route)  103 us
    ppermute x30, starting transfers between devices, from_behind(): return lax.ppermute(block, axis, route)  83.7 us
    all_gather x1, waiting for transfers between devices, body(): lax.all_gather(rank_local, 'dp', axis=1, tiled=True)  67.8 us
    scatter x30, other arithmetic, put_block(): return store.at[layer_idx, position].set(jnp.where(usable, value, previous))  47 us
    all_gather x1, waiting for transfers between devices, body(): lax.all_gather(rank_grad_local, 'dp', axis=1, tiled=True)  46.8 us
    another operation x30, other arithmetic  41.5 us
    dot_general x15, matrix products, layer_forward(): lax.dot_general(normed, down_weight, (((1,), (1,)), ((), ())), preferred_...  29.6 us
    dot_general x15, matrix products, layer_backward(): lax.dot_general(grad_rows, up_weight, (((1,), (1,)), ((), ())), preferred...  27.9 us
  transfers between devices with their start and end apart: 36, of which 35 were waited for; matrix products, arithmetic and copies ran while one was open for 6% of the time, Pallas kernels for 0%

commit v1 on v0

--- a/solution.py
+++ b/solution.py
@@ -143,7 +143,9 @@
     rank_grad_local = records[1].reshape(layer_stack, token_count, rank_columns)
     rank_every, rank_grad_every = (
         lax.all_gather(rank_local, "dp", axis=1, tiled=True),
-        lax.all_gather(rank_grad_local, "dp", axis=1, tiled=True),
+        jnp.concatenate(
+            lax.all_to_all(jnp.stack([rank_grad_local] * lax.axis_size("dp")), "dp", 0, 0), axis=1
+        ),
     )
     rank_every = rank_every.reshape(layer_stack, pieces, token_count, rank_columns)
     rank_grad_every = rank_grad_every.reshape(layer_stack, pieces, token_count, rank_columns)

time: 662 us -> 591 us (0.89)
  waiting for transfers between devices: 256 us -> 196 us
  matrix products: 89.6 us -> 75.6 us
  starting transfers between devices: 126 us -> 140 us
  other arithmetic: 98.3 us -> 89.9 us
    all_gather x1 -> x0, waiting for transfers between devices: 46.8 us -> none  [body(): lax.all_gather(rank_grad_local, 'dp', axis=1, tiled=True)]
    all_to_all x1, waiting for transfers between devices: 24.1 us -> 0.01 us  [body(): lax.all_to_all(normed_all, 'dp', split_axis=2, concat_axis=1, tiled=True)]
    all_to_all x0 -> x1, waiting for transfers between devices: none -> 23.6 us  [body(): lax.all_to_all(jnp.stack([rank_grad_local] * lax.axis_size('dp')), 'dp',...]
    dot_general x15, matrix products: 27.9 us -> 13.1 us  [layer_backward(): lax.dot_general(grad_rows, up_weight, (((1,), (1,)), ((), ())), preferred...]
    all_gather x1, waiting for transfers between devices: 67.8 us -> 54.8 us  [body(): lax.all_gather(rank_local, 'dp', axis=1, tiled=True)]
    all_to_all x0 -> x1, starting transfers between devices: none -> 12.9 us  [body(): lax.all_to_all(jnp.stack([rank_grad_local] * lax.axis_size('dp')), 'dp',...]
    another operation x30, other arithmetic: 41.5 us -> 32.6 us
  transfers between devices with their start and end apart: 36 -> 36, of which waited for: 35 -> 34; matrix products, arithmetic and copies ran while one was open for 6% -> 17% of each run, Pallas kernels for 0% -> 0%
where the time goes in v1:
time: 591 us; the launch traced here: 586 us
  waiting for transfers between devices  196 us (33%)
  starting transfers between devices  140 us (24%)
  other arithmetic  89.9 us (15%)
  matrix products  75.6 us (13%)
  local copies, waits for them, and re-layouts  51.5 us (9%)
  loops' own time  19.4 us (3%)
  between operations  14.4 us (2%)
    ppermute x30, waiting for transfers between devices, from_behind(): return lax.ppermute(block, axis, route)  103 us
    ppermute x30, starting transfers between devices, from_behind(): return lax.ppermute(block, axis, route)  84 us
    all_gather x1, waiting for transfers between devices, body(): lax.all_gather(rank_local, 'dp', axis=1, tiled=True)  54.8 us
    scatter x30, other arithmetic, put_block(): return store.at[layer_idx, position].set(jnp.where(usable, value, previous))  48.5 us
    another operation x30, other arithmetic  32.6 us
    dot_general x15, matrix products, layer_forward(): lax.dot_general(normed, down_weight, (((1,), (1,)), ((), ())), preferred_...  30.3 us
    all_to_all x1, waiting for transfers between devices, body(): lax.all_to_all(jnp.stack([rank_grad_local] * lax.axis_size('dp')), 'dp',...  23.6 us
    dot_general x15, matrix products, layer_forward(): jnp.dot(rank_row_values, up_weight, preferred_element_type=jnp.float32)  18.8 us
  transfers between devices with their start and end apart: 36, of which 34 were waited for; matrix products, arithmetic and copies ran while one was open for 17% of the time, Pallas kernels for 0%

profile of v1, /device:TPU:2, one launch (start us, length us, event | category | flops | bytes accessed | tf_op | source)
XLA Modules:
  0.0 586.4 jit_solution(15111999495730066679)
XLA Ops:
  8.1 210.2 %while.35 = (s32[]{:T(128)}, bf16[16,4096]{1,0:T(8,128)(2,1)S(1)}, bf16[1,8,16,4096]{3,2,1,0:T(8,128)(2,1)S(1)}, bf16[1,8,16,64]{3,2,1,0:T(8,128)(2,1)S(1)}, pre...) while((s32[]{:T(128)}, bf16[16,4096]{1,0:T(8,128)(2,1)S(1)}, ...), condition=%wide.region_4.5_spmd, body=%wide.region_1.4_spmd.sunk | while | flops 17633332 | bytes 3036152 | solution.py:100
  17.8 4.4 collective-permute-done
  31.8 4.4 collective-permute-done
  45.9 4.4 collective-permute-done
  59.9 4.4 collective-permute-done
  73.9 4.4 collective-permute-done
  87.9 4.4 collective-permute-done
  101.9 4.4 collective-permute-done
  115.9 4.4 collective-permute-done
  129.9 4.4 collective-permute-done
  143.9 4.4 collective-permute-done
  157.9 4.4 collective-permute-done
  171.9 4.4 collective-permute-done
  185.9 4.4 collective-permute-done
  199.9 4.4 collective-permute-done
  214.0 4.4 collective-permute-done
  218.9 3.3 reshape.319
  222.2 4.0 copy.50
  226.3 16.9 %all-to-all-start.1 = ((bf16[1,128,64,64]{1,3,0,2:T(8,128)(2,1)}), bf16[1,128,64,64]{1,3,0,2:T(8,128)(2,1)}, u32[]{:S(2)}, u32[]{:S(2)}) async-start(bf16[1,128,64,64]{1,3,0,2:T(8,128)(2,1)} %copy.50), calls=%async_computation.1 | async-start | bytes 2097152 | tf_op jit(solution)/shard_map/all_to_all | solution.py:137
  243.3 170.2 %while.36 = (s32[]{:T(128)}, bf16[16,4096]{1,0:T(8,128)(2,1)S(1)}, bf16[1,8,16,4096]{3,2,1,0:T(8,128)(2,1)S(1)}, bf16[1,8,16,64]{3,2,1,0:T(8,128)(2,1)S(1)}, pre...) while((s32[]{:T(128)}, bf16[16,4096]{1,0:T(8,128)(2,1)S(1)}, ...), condition=%wide.region_9.10_spmd, body=%wide.region_5.9_spmd.sunk | while | flops 17962036 | bytes 3822476 | solution.py:128
  258.1 4.2 collective-permute-start.1
  262.3 2.5 collective-permute-done.1
  269.9 3.8 collective-permute-start.1
  273.7 2.5 collective-permute-done.1
  281.4 3.8 collective-permute-start.1
  285.2 2.5 collective-permute-done.1
  292.8 3.8 collective-permute-start.1
  304.3 3.8 collective-permute-start.1
  315.7 3.8 collective-permute-start.1
  327.2 3.8 collective-permute-start.1
  331.0 2.5 collective-permute-done.1
  338.6 3.8 collective-permute-start.1
  342.4 2.5 collective-permute-done.1
  350.1 3.8 collective-permute-start.1
  361.5 3.8 collective-permute-start.1
  373.0 3.8 collective-permute-start.1
  384.4 3.8 collective-permute-start.1
  395.8 3.8 collective-permute-start.1
  407.3 3.8 collective-permute-start.1
  414.9 12.9 %all-to-all-start = ((bf16[64,1,128,64]{2,3,1,0:T(8,128)(2,1)}), bf16[64,1,128,64]{2,3,1,0:T(8,128)(2,1)}, u32[]{:S(2)}, u32[]{:S(2)}) async-start(bf16[64,1,128,64]{2,3,1,0:T(8,128)(2,1)} %stack.3), calls=%async_computation | async-start | bytes 2097152 | tf_op jit(solution)/shard_map/all_to_all | solution.py:147
  430.9 3.0 copy.56
  433.9 23.6 %all-to-all-done = bf16[64,1,128,64]{2,3,1,0:T(8,128)(2,1)} async-done(((bf16[64,1,128,64]{2,3,1,0:T(8,128)(2,1)}), bf16[64,1,128,64]{2,3,1,0:T(8,128)(2,1)}, u32[]{:S(2)}, u32[]{:S(2)}) %all-to-all-start) | async-done | bytes 1048608 | tf_op jit(solution)/shard_map/all_to_all | solution.py:147
  457.5 8.6 %all-to-all-start.3 = ((bf16[1,128,64,64]{1,3,0,2:T(8,128)(2,1)}), bf16[1,128,64,64]{1,3,0,2:T(8,128)(2,1)}, u32[]{:S(2)}, u32[]{:S(2)}) async-start(bf16[1,128,64,64]{1,3,0,2:T(8,128)(2,1)} %copy.56), calls=%async_computation.3 | async-start | bytes 2097152 | tf_op jit(solution)/shard_map/all_to_all | solution.py:138
  476.6 54.8 %all-gather.2.cloned.1.call-done = bf16[1,8192,64]{1,2,0:T(8,128)(2,1)} async-done(((bf16[1,128,64]{1,2,0:T(8,128)(2,1)}), bf16[1,8192,64]{1,2,0:T(8,128)(2,1)}) %all-gather.2.cloned.1.call-update) | async-done | bytes 1048592 | tf_op jit(solution)/shard_map/all_gather | solution.py:145
  532.9 8.0 %all-to-all-start.2 = ((bf16[64,2,1024]{2,1,0:T(2,128)(2,1)}), bf16[64,2,1024]{2,1,0:T(2,128)(2,1)S(1)}, u32[]{:S(2)}, u32[]{:S(2)}) async-start(bf16[64,2,1024]{2,1,0:T(2,128)(2,1)} %reshape.335), calls=%async_computation.2 | async-start | bytes 524288 | tf_op jit(solution)/shard_map/all_to_all | solution.py:178
  551.2 3.0 all-to-all-done.2
  554.3 9.5 %all-to-all-start.4 = ((bf16[64,2,1024]{2,1,0:T(2,128)(2,1)}), bf16[64,2,1024]{2,1,0:T(2,128)(2,1)S(1)}, u32[]{:S(2)}, u32[]{:S(2)}) async-start(bf16[64,2,1024]{2,1,0:T(2,128)(2,1)} %reshape.337), calls=%async_computation.4 | async-start | bytes 524288 | tf_op jit(solution)/shard_map/all_to_all | solution.py:181
  566.0 11.3 %all-to-all-done.4 = bf16[64,2,1024]{2,1,0:T(2,128)(2,1)S(1)} async-done(((bf16[64,2,1024]{2,1,0:T(2,128)(2,1)}), bf16[64,2,1024]{2,1,0:T(2,128)(2,1)S(1)}, u32[]{:S(2)}, u32[]{:S(2)}) %all-to-all-start.4) | async-done | bytes 262176 | tf_op jit(solution)/shard_map/all_to_all | solution.py:181
  (381 shorter events, 262.5 us)
Async XLA Ops:
  15.8 6.3 %collective-permute-start = (bf16[16,4096]{1,0:T(8,128)(2,1)S(1)}, bf16[16,4096]{1,0:T(8,128)(2,1)S(1)}, u32[]{:S(2)}, u32[]{:S(2)}) collective-permute-start(bf16[16,4096]{1,0:T(8,128)(2,1)S(1)} %fusion.84), channel_id=1, source_target_pairs={{0,64},{64,128},{128,192},{192,256},{256,320},{320,384},{384,448},... | collective-permute-start | bytes 393224 | tf_op jit(solution)/shard_map/while/body/eval_jaxpr/ppermute | solution.py:13
  29.9 6.4 %collective-permute-start = (bf16[16,4096]{1,0:T(8,128)(2,1)S(1)}, bf16[16,4096]{1,0:T(8,128)(2,1)S(1)}, u32[]{:S(2)}, u32[]{:S(2)}) collective-permute-start(bf16[16,4096]{1,0:T(8,128)(2,1)S(1)} %fusion.84), channel_id=1, source_target_pairs={{0,64},{64,128},{128,192},{192,256},{256,320},{320,384},{384,448},... | collective-permute-start | bytes 393224 | tf_op jit(solution)/shard_map/while/body/eval_jaxpr/ppermute | solution.py:13
  44.0 6.3 %collective-permute-start = (bf16[16,4096]{1,0:T(8,128)(2,1)S(1)}, bf16[16,4096]{1,0:T(8,128)(2,1)S(1)}, u32[]{:S(2)}, u32[]{:S(2)}) collective-permute-start(bf16[16,4096]{1,0:T(8,128)(2,1)S(1)} %fusion.84), channel_id=1, source_target_pairs={{0,64},{64,128},{128,192},{192,256},{256,320},{320,384},{384,448},... | collective-permute-start | bytes 393224 | tf_op jit(solution)/shard_map/while/body/eval_jaxpr/ppermute | solution.py:13
  58.0 6.3 %collective-permute-start = (bf16[16,4096]{1,0:T(8,128)(2,1)S(1)}, bf16[16,4096]{1,0:T(8,128)(2,1)S(1)}, u32[]{:S(2)}, u32[]{:S(2)}) collective-permute-start(bf16[16,4096]{1,0:T(8,128)(2,1)S(1)} %fusion.84), channel_id=1, source_target_pairs={{0,64},{64,128},{128,192},{192,256},{256,320},{320,384},{384,448},... | collective-permute-start | bytes 393224 | tf_op jit(solution)/shard_map/while/body/eval_jaxpr/ppermute | solution.py:13
  72.0 6.3 %collective-permute-start = (bf16[16,4096]{1,0:T(8,128)(2,1)S(1)}, bf16[16,4096]{1,0:T(8,128)(2,1)S(1)}, u32[]{:S(2)}, u32[]{:S(2)}) collective-permute-start(bf16[16,4096]{1,0:T(8,128)(2,1)S(1)} %fusion.84), channel_id=1, source_target_pairs={{0,64},{64,128},{128,192},{192,256},{256,320},{320,384},{384,448},... | collective-permute-start | bytes 393224 | tf_op jit(solution)/shard_map/while/body/eval_jaxpr/ppermute | solution.py:13
  86.0 6.3 %collective-permute-start = (bf16[16,4096]{1,0:T(8,128)(2,1)S(1)}, bf16[16,4096]{1,0:T(8,128)(2,1)S(1)}, u32[]{:S(2)}, u32[]{:S(2)}) collective-permute-start(bf16[16,4096]{1,0:T(8,128)(2,1)S(1)} %fusion.84), channel_id=1, source_target_pairs={{0,64},{64,128},{128,192},{192,256},{256,320},{320,384},{384,448},... | collective-permute-start | bytes 393224 | tf_op jit(solution)/shard_map/while/body/eval_jaxpr/ppermute | solution.py:13
  100.0 6.3 %collective-permute-start = (bf16[16,4096]{1,0:T(8,128)(2,1)S(1)}, bf16[16,4096]{1,0:T(8,128)(2,1)S(1)}, u32[]{:S(2)}, u32[]{:S(2)}) collective-permute-start(bf16[16,4096]{1,0:T(8,128)(2,1)S(1)} %fusion.84), channel_id=1, source_target_pairs={{0,64},{64,128},{128,192},{192,256},{256,320},{320,384},{384,448},... | collective-permute-start | bytes 393224 | tf_op jit(solution)/shard_map/while/body/eval_jaxpr/ppermute | solution.py:13
  114.0 6.3 %collective-permute-start = (bf16[16,4096]{1,0:T(8,128)(2,1)S(1)}, bf16[16,4096]{1,0:T(8,128)(2,1)S(1)}, u32[]{:S(2)}, u32[]{:S(2)}) collective-permute-start(bf16[16,4096]{1,0:T(8,128)(2,1)S(1)} %fusion.84), channel_id=1, source_target_pairs={{0,64},{64,128},{128,192},{192,256},{256,320},{320,384},{384,448},... | collective-permute-start | bytes 393224 | tf_op jit(solution)/shard_map/while/body/eval_jaxpr/ppermute | solution.py:13
  128.0 6.3 %collective-permute-start = (bf16[16,4096]{1,0:T(8,128)(2,1)S(1)}, bf16[16,4096]{1,0:T(8,128)(2,1)S(1)}, u32[]{:S(2)}, u32[]{:S(2)}) collective-permute-start(bf16[16,4096]{1,0:T(8,128)(2,1)S(1)} %fusion.84), channel_id=1, source_target_pairs={{0,64},{64,128},{128,192},{192,256},{256,320},{320,384},{384,448},... | collective-permute-start | bytes 393224 | tf_op jit(solution)/shard_map/while/body/eval_jaxpr/ppermute | solution.py:13
  142.0 6.3 %collective-permute-start = (bf16[16,4096]{1,0:T(8,128)(2,1)S(1)}, bf16[16,4096]{1,0:T(8,128)(2,1)S(1)}, u32[]{:S(2)}, u32[]{:S(2)}) collective-permute-start(bf16[16,4096]{1,0:T(8,128)(2,1)S(1)} %fusion.84), channel_id=1, source_target_pairs={{0,64},{64,128},{128,192},{192,256},{256,320},{320,384},{384,448},... | collective-permute-start | bytes 393224 | tf_op jit(solution)/shard_map/while/body/eval_jaxpr/ppermute | solution.py:13
  156.0 6.3 %collective-permute-start = (bf16[16,4096]{1,0:T(8,128)(2,1)S(1)}, bf16[16,4096]{1,0:T(8,128)(2,1)S(1)}, u32[]{:S(2)}, u32[]{:S(2)}) collective-permute-start(bf16[16,4096]{1,0:T(8,128)(2,1)S(1)} %fusion.84), channel_id=1, source_target_pairs={{0,64},{64,128},{128,192},{192,256},{256,320},{320,384},{384,448},... | collective-permute-start | bytes 393224 | tf_op jit(solution)/shard_map/while/body/eval_jaxpr/ppermute | solution.py:13
  170.0 6.3 %collective-permute-start = (bf16[16,4096]{1,0:T(8,128)(2,1)S(1)}, bf16[16,4096]{1,0:T(8,128)(2,1)S(1)}, u32[]{:S(2)}, u32[]{:S(2)}) collective-permute-start(bf16[16,4096]{1,0:T(8,128)(2,1)S(1)} %fusion.84), channel_id=1, source_target_pairs={{0,64},{64,128},{128,192},{192,256},{256,320},{320,384},{384,448},... | collective-permute-start | bytes 393224 | tf_op jit(solution)/shard_map/while/body/eval_jaxpr/ppermute | solution.py:13
  184.0 6.3 %collective-permute-start = (bf16[16,4096]{1,0:T(8,128)(2,1)S(1)}, bf16[16,4096]{1,0:T(8,128)(2,1)S(1)}, u32[]{:S(2)}, u32[]{:S(2)}) collective-permute-start(bf16[16,4096]{1,0:T(8,128)(2,1)S(1)} %fusion.84), channel_id=1, source_target_pairs={{0,64},{64,128},{128,192},{192,256},{256,320},{320,384},{384,448},... | collective-permute-start | bytes 393224 | tf_op jit(solution)/shard_map/while/body/eval_jaxpr/ppermute | solution.py:13
  198.0 6.3 %collective-permute-start = (bf16[16,4096]{1,0:T(8,128)(2,1)S(1)}, bf16[16,4096]{1,0:T(8,128)(2,1)S(1)}, u32[]{:S(2)}, u32[]{:S(2)}) collective-permute-start(bf16[16,4096]{1,0:T(8,128)(2,1)S(1)} %fusion.84), channel_id=1, source_target_pairs={{0,64},{64,128},{128,192},{192,256},{256,320},{320,384},{384,448},... | collective-permute-start | bytes 393224 | tf_op jit(solution)/shard_map/while/body/eval_jaxpr/ppermute | solution.py:13
  212.0 6.3 %collective-permute-start = (bf16[16,4096]{1,0:T(8,128)(2,1)S(1)}, bf16[16,4096]{1,0:T(8,128)(2,1)S(1)}, u32[]{:S(2)}, u32[]{:S(2)}) collective-permute-start(bf16[16,4096]{1,0:T(8,128)(2,1)S(1)} %fusion.84), channel_id=1, source_target_pairs={{0,64},{64,128},{128,192},{192,256},{256,320},{320,384},{384,448},... | collective-permute-start | bytes 393224 | tf_op jit(solution)/shard_map/while/body/eval_jaxpr/ppermute | solution.py:13
  226.2 17.1 %copy-start = (bf16[1,1,1,2,32,4096]{5,4,3,2,1,0:T(8,128)(2,1)S(1)}, bf16[1,1,1,2,32,4096]{5,4,3,2,1,0:T(8,128)(2,1)}, u32[]{:S(2)}) copy-start(bf16[1,1,1,2,32,4096]{5,4,3,2,1,0:T(8,128)(2,1)} %get-tuple-element.607) | copy-start | bytes 1572868
  226.2 17.1 %copy-start.1 = (bf16[1,1,1,2,32,4096]{5,4,3,2,1,0:T(8,128)(2,1)S(1)}, bf16[1,1,1,2,32,4096]{5,4,3,2,1,0:T(8,128)(2,1)}, u32[]{:S(2)}) copy-start(bf16[1,1,1,2,32,4096]{5,4,3,2,1,0:T(8,128)(2,1)} %get-tuple-element.608) | copy-start | bytes 1572868
  226.2 17.1 %copy-start.2 = (s32[4]{0:T(128)S(1)}, s32[4]{0:T(128)}, u32[]{:S(2)}) copy-start(s32[4]{0:T(128)} %get-tuple-element.619) | copy-start | bytes 52
  226.3 187.4 %all-to-all-start.1 = ((bf16[1,128,64,64]{1,3,0,2:T(8,128)(2,1)}), bf16[1,128,64,64]{1,3,0,2:T(8,128)(2,1)}, u32[]{:S(2)}, u32[]{:S(2)}) async-start(bf16[1,128,64,64]{1,3,0,2:T(8,128)(2,1)} %copy.50), calls=%async_computation.1 | async-start | bytes 2097152 | tf_op jit(solution)/shard_map/all_to_all | solution.py:137
  248.5 4.4 collective-permute-start.1
  258.1 6.7 %collective-permute-start.1 = (bf16[16,4096]{1,0:T(8,128)(2,1)S(1)}, bf16[16,4096]{1,0:T(8,128)(2,1)S(1)}, u32[]{:S(2)}, u32[]{:S(2)}) collective-permute-start(bf16[16,4096]{1,0:T(8,128)(2,1)S(1)} %fusion.93), channel_id=1, source_target_pairs={{64,0},{128,64},{192,128},{256,192},{320,256},{384,320},{448,384},... | collective-permute-start | bytes 393224 | tf_op jit(solution)/shard_map/while/body/eval_jaxpr/ppermute | solution.py:13
  269.9 6.3 %collective-permute-start.1 = (bf16[16,4096]{1,0:T(8,128)(2,1)S(1)}, bf16[16,4096]{1,0:T(8,128)(2,1)S(1)}, u32[]{:S(2)}, u32[]{:S(2)}) collective-permute-start(bf16[16,4096]{1,0:T(8,128)(2,1)S(1)} %fusion.93), channel_id=1, source_target_pairs={{64,0},{128,64},{192,128},{256,192},{320,256},{384,320},{448,384},... | collective-permute-start | bytes 393224 | tf_op jit(solution)/shard_map/while/body/eval_jaxpr/ppermute | solution.py:13
  281.4 6.3 %collective-permute-start.1 = (bf16[16,4096]{1,0:T(8,128)(2,1)S(1)}, bf16[16,4096]{1,0:T(8,128)(2,1)S(1)}, u32[]{:S(2)}, u32[]{:S(2)}) collective-permute-start(bf16[16,4096]{1,0:T(8,128)(2,1)S(1)} %fusion.93), channel_id=1, source_target_pairs={{64,0},{128,64},{192,128},{256,192},{320,256},{384,320},{448,384},... | collective-permute-start | bytes 393224 | tf_op jit(solution)/shard_map/while/body/eval_jaxpr/ppermute | solution.py:13
  292.8 6.3 %collective-permute-start.1 = (bf16[16,4096]{1,0:T(8,128)(2,1)S(1)}, bf16[16,4096]{1,0:T(8,128)(2,1)S(1)}, u32[]{:S(2)}, u32[]{:S(2)}) collective-permute-start(bf16[16,4096]{1,0:T(8,128)(2,1)S(1)} %fusion.93), channel_id=1, source_target_pairs={{64,0},{128,64},{192,128},{256,192},{320,256},{384,320},{448,384},... | collective-permute-start | bytes 393224 | tf_op jit(solution)/shard_map/while/body/eval_jaxpr/ppermute | solution.py:13
  304.3 6.3 %collective-permute-start.1 = (bf16[16,4096]{1,0:T(8,128)(2,1)S(1)}, bf16[16,4096]{1,0:T(8,128)(2,1)S(1)}, u32[]{:S(2)}, u32[]{:S(2)}) collective-permute-start(bf16[16,4096]{1,0:T(8,128)(2,1)S(1)} %fusion.93), channel_id=1, source_target_pairs={{64,0},{128,64},{192,128},{256,192},{320,256},{384,320},{448,384},... | collective-permute-start | bytes 393224 | tf_op jit(solution)/shard_map/while/body/eval_jaxpr/ppermute | solution.py:13
  315.7 6.3 %collective-permute-start.1 = (bf16[16,4096]{1,0:T(8,128)(2,1)S(1)}, bf16[16,4096]{1,0:T(8,128)(2,1)S(1)}, u32[]{:S(2)}, u32[]{:S(2)}) collective-permute-start(bf16[16,4096]{1,0:T(8,128)(2,1)S(1)} %fusion.93), channel_id=1, source_target_pairs={{64,0},{128,64},{192,128},{256,192},{320,256},{384,320},{448,384},... | collective-permute-start | bytes 393224 | tf_op jit(solution)/shard_map/while/body/eval_jaxpr/ppermute | solution.py:13
  327.2 6.3 %collective-permute-start.1 = (bf16[16,4096]{1,0:T(8,128)(2,1)S(1)}, bf16[16,4096]{1,0:T(8,128)(2,1)S(1)}, u32[]{:S(2)}, u32[]{:S(2)}) collective-permute-start(bf16[16,4096]{1,0:T(8,128)(2,1)S(1)} %fusion.93), channel_id=1, source_target_pairs={{64,0},{128,64},{192,128},{256,192},{320,256},{384,320},{448,384},... | collective-permute-start | bytes 393224 | tf_op jit(solution)/shard_map/while/body/eval_jaxpr/ppermute | solution.py:13
  338.6 6.3 %collective-permute-start.1 = (bf16[16,4096]{1,0:T(8,128)(2,1)S(1)}, bf16[16,4096]{1,0:T(8,128)(2,1)S(1)}, u32[]{:S(2)}, u32[]{:S(2)}) collective-permute-start(bf16[16,4096]{1,0:T(8,128)(2,1)S(1)} %fusion.93), channel_id=1, source_target_pairs={{64,0},{128,64},{192,128},{256,192},{320,256},{384,320},{448,384},... | collective-permute-start | bytes 393224 | tf_op jit(solution)/shard_map/while/body/eval_jaxpr/ppermute | solution.py:13
  350.1 6.3 %collective-permute-start.1 = (bf16[16,4096]{1,0:T(8,128)(2,1)S(1)}, bf16[16,4096]{1,0:T(8,128)(2,1)S(1)}, u32[]{:S(2)}, u32[]{:S(2)}) collective-permute-start(bf16[16,4096]{1,0:T(8,128)(2,1)S(1)} %fusion.93), channel_id=1, source_target_pairs={{64,0},{128,64},{192,128},{256,192},{320,256},{384,320},{448,384},... | collective-permute-start | bytes 393224 | tf_op jit(solution)/shard_map/while/body/eval_jaxpr/ppermute | solution.py:13
  361.5 6.3 %collective-permute-start.1 = (bf16[16,4096]{1,0:T(8,128)(2,1)S(1)}, bf16[16,4096]{1,0:T(8,128)(2,1)S(1)}, u32[]{:S(2)}, u32[]{:S(2)}) collective-permute-start(bf16[16,4096]{1,0:T(8,128)(2,1)S(1)} %fusion.93), channel_id=1, source_target_pairs={{64,0},{128,64},{192,128},{256,192},{320,256},{384,320},{448,384},... | collective-permute-start | bytes 393224 | tf_op jit(solution)/shard_map/while/body/eval_jaxpr/ppermute | solution.py:13
  373.0 6.3 %collective-permute-start.1 = (bf16[16,4096]{1,0:T(8,128)(2,1)S(1)}, bf16[16,4096]{1,0:T(8,128)(2,1)S(1)}, u32[]{:S(2)}, u32[]{:S(2)}) collective-permute-start(bf16[16,4096]{1,0:T(8,128)(2,1)S(1)} %fusion.93), channel_id=1, source_target_pairs={{64,0},{128,64},{192,128},{256,192},{320,256},{384,320},{448,384},... | collective-permute-start | bytes 393224 | tf_op jit(solution)/shard_map/while/body/eval_jaxpr/ppermute | solution.py:13
  384.4 6.3 %collective-permute-start.1 = (bf16[16,4096]{1,0:T(8,128)(2,1)S(1)}, bf16[16,4096]{1,0:T(8,128)(2,1)S(1)}, u32[]{:S(2)}, u32[]{:S(2)}) collective-permute-start(bf16[16,4096]{1,0:T(8,128)(2,1)S(1)} %fusion.93), channel_id=1, source_target_pairs={{64,0},{128,64},{192,128},{256,192},{320,256},{384,320},{448,384},... | collective-permute-start | bytes 393224 | tf_op jit(solution)/shard_map/while/body/eval_jaxpr/ppermute | solution.py:13
  395.8 6.3 %collective-permute-start.1 = (bf16[16,4096]{1,0:T(8,128)(2,1)S(1)}, bf16[16,4096]{1,0:T(8,128)(2,1)S(1)}, u32[]{:S(2)}, u32[]{:S(2)}) collective-permute-start(bf16[16,4096]{1,0:T(8,128)(2,1)S(1)} %fusion.93), channel_id=1, source_target_pairs={{64,0},{128,64},{192,128},{256,192},{320,256},{384,320},{448,384},... | collective-permute-start | bytes 393224 | tf_op jit(solution)/shard_map/while/body/eval_jaxpr/ppermute | solution.py:13
  407.3 6.3 %collective-permute-start.1 = (bf16[16,4096]{1,0:T(8,128)(2,1)S(1)}, bf16[16,4096]{1,0:T(8,128)(2,1)S(1)}, u32[]{:S(2)}, u32[]{:S(2)}) collective-permute-start(bf16[16,4096]{1,0:T(8,128)(2,1)S(1)} %fusion.93), channel_id=1, source_target_pairs={{64,0},{128,64},{192,128},{256,192},{320,256},{384,320},{448,384},... | collective-permute-start | bytes 393224 | tf_op jit(solution)/shard_map/while/body/eval_jaxpr/ppermute | solution.py:13
  414.9 42.6 %all-to-all-start = ((bf16[64,1,128,64]{2,3,1,0:T(8,128)(2,1)}), bf16[64,1,128,64]{2,3,1,0:T(8,128)(2,1)}, u32[]{:S(2)}, u32[]{:S(2)}) async-start(bf16[64,1,128,64]{2,3,1,0:T(8,128)(2,1)} %stack.3), calls=%async_computation | async-start | bytes 2097152 | tf_op jit(solution)/shard_map/all_to_all | solution.py:147
  427.8 103.6 %all-gather.2.cloned.1.call-start = ((), (), s32[]{:S(2)}) async-start(), calls=%async_computation.5 | async-start | bytes 1064960 | tf_op jit(solution)/shard_map/all_gather | solution.py:145
  430.9 35.2 %copy-start.3 = (s32[64,2]{0,1:T(2,128)S(1)}, s32[64,2]{0,1:T(2,128)}, u32[]{:S(2)}) copy-start(s32[64,2]{0,1:T(2,128)} %param.22) | copy-start | bytes 1540
  430.9 35.2 %copy-start.4 = (s32[64]{0:T(128)S(1)}, s32[64]{0:T(128)}, u32[]{:S(2)}) copy-start(s32[64]{0:T(128)} %param.23) | copy-start | bytes 772
  457.5 75.4 %all-to-all-start.3 = ((bf16[1,128,64,64]{1,3,0,2:T(8,128)(2,1)}), bf16[1,128,64,64]{1,3,0,2:T(8,128)(2,1)}, u32[]{:S(2)}, u32[]{:S(2)}) async-start(bf16[1,128,64,64]{1,3,0,2:T(8,128)(2,1)} %copy.56), calls=%async_computation.3 | async-start | bytes 2097152 | tf_op jit(solution)/shard_map/all_to_all | solution.py:138
  532.9 21.4 %all-to-all-start.2 = ((bf16[64,2,1024]{2,1,0:T(2,128)(2,1)}), bf16[64,2,1024]{2,1,0:T(2,128)(2,1)S(1)}, u32[]{:S(2)}, u32[]{:S(2)}) async-start(bf16[64,2,1024]{2,1,0:T(2,128)(2,1)} %reshape.335), calls=%async_computation.2 | async-start | bytes 524288 | tf_op jit(solution)/shard_map/all_to_all | solution.py:178
  554.3 23.1 %all-to-all-start.4 = ((bf16[64,2,1024]{2,1,0:T(2,128)(2,1)}), bf16[64,2,1024]{2,1,0:T(2,128)(2,1)S(1)}, u32[]{:S(2)}, u32[]{:S(2)}) async-start(bf16[64,2,1024]{2,1,0:T(2,128)(2,1)} %reshape.337), calls=%async_computation.4 | async-start | bytes 524288 | tf_op jit(solution)/shard_map/all_to_all | solution.py:181
Sparse Core Ops, SparseCore 0:
  432.2 99.1 all-gather.1
